TPU v7x, 32 devices: a whole 2x2x4 slice. The times are simulated.
32 devices in a mesh: groups: 2 (over y), qry: 4 (over x, core), ref: 4 (over z).
Axes of the slice: x: 2, y: 2, z: 4, core: 2. Of those that a mesh axis runs over, the one named last changes fastest.
Arguments:
- query_feats: bfloat16 [1024, 9, 3840], P(('groups', 'qry')), parts along dimension 0, may hold values from -6 to 6
- ref_feats: bfloat16 [256, 4, 9, 3840], P(('groups', 'ref'), 'qry'), parts along dimension 0, may hold values from -6 to 6
- pair_table: int32 [8, 4], P('groups'), parts along dimension 0, may hold values from 0 to 1, as said below
- lengths: int32 [4], P('groups'), parts along dimension 0, may hold values from 1 to 96, 128 in all
- query_len: int32 [2], P('groups'), parts along dimension 0, may hold values from 64 to 128
- conv1_weight: float32 [3, 3, 32], replicated, may hold values from -2 to 2
- conv1_bias: float32 [32], replicated, may hold values from -3 to 3
- conv2_weight: bfloat16 [3, 3, 64, 32], replicated, may hold values from -0.375 to 0.375
- conv2_bias: float32 [64], replicated, may hold values from -3 to 3
- conv3_weight: bfloat16 [3, 3, 128, 64], replicated, may hold values from -0.25 to 0.25
- conv3_bias: float32 [128], replicated, may hold values from -3 to 3
- conv4_weight: bfloat16 [128], replicated, may hold values from -0.5 to 0.5
- conv4_bias: float32 [1], replicated, may hold values from -3 to 3
Outputs:
- score_map: float32 [256, 128], P(('groups', 'qry'), 'ref'), parts along dimension 0
- video_scores: float32 [4], P('groups'), parts along dimension 0
There are 2 independent parts, one for each index of `groups`. A program takes and returns all parts, laid end to end along the dimension named above; an argument that names none is the same for every part. Nothing has to cross between parts.
Inputs may be any that keep to these rules, and one draw needn't show every extreme that they name: `pair_table`: in each row, at most 1 of the 1 tiles in the block of one index of ref are 1, and some such block holds exactly 1 in every draw.
All inputs are finite; a program needn't handle non-finite values.
Results may differ from a plain program's by a relative error of at most 0.01.
Values may be sent and summed in bfloat16 or wider, within the bound.
A program may use at most 128 MiB of HBM per device.

v0:
```python
import math

import jax
import jax.numpy as jnp
from jax import lax
from jax.sharding import PartitionSpec as P

MOST = 1


def padded_2(block, sides, width):
    for axis, dim in sides:
        count = lax.axis_size(axis)
        forward = [(i, i + 1) for i in range(count - 1)]
        backward = [(target, source) for source, target in forward]
        low = lax.ppermute(
            lax.slice_in_dim(block, block.shape[dim] - width, None, axis=dim), axis, forward
        )
        high = lax.ppermute(lax.slice_in_dim(block, 0, width, axis=dim), axis, backward)
        block = jnp.concatenate([low, block, high], axis=dim)
    return block


def slot_table(mask, most):
    width = mask.shape[-1]
    ranking = jnp.cumsum(mask, axis=-1) - 1
    slot_ids = jnp.arange(most, dtype=jnp.int32)
    chosen = (mask[..., None, :] == 1) & (ranking[..., None, :] == slot_ids[:, None])
    picked = jnp.sum(jnp.where(chosen, jnp.arange(width, dtype=jnp.int32), 0), axis=-1)
    return (chosen, picked)


def frame_sims(query_mat, ref_mat, regions):
    products = lax.dot_general(
        query_mat, ref_mat, (((1,), (1,)), ((), ())), preferred_element_type=jnp.float32
    )
    frames = query_mat.shape[0] // regions
    others = ref_mat.shape[0] // regions
    best = jnp.max(products.reshape(frames, regions, others, regions), axis=3)
    return jnp.sum(best, axis=1) * (1.0 / (regions * math.sqrt(query_mat.shape[1])))


def conv_layer(padded, weights, bias, block_rows, use_pool):
    channels = padded.shape[0]
    height = padded.shape[1] - 2
    width = padded.shape[2] - 2
    block_rows = math.gcd(height, block_rows)
    outputs = weights.shape[0]
    accuracy = lax.Precision.HIGHEST if padded.dtype == jnp.float32 else None

    def one_block(position):
        window = lax.dynamic_slice_in_dim(padded, position * block_rows, block_rows + 2, 1)
        stacked = jnp.concatenate(
            [
                window[:, shift_row : shift_row + block_rows, shift_col : shift_col + width]
                for shift_row in range(3)
                for shift_col in range(3)
            ],
            axis=0,
        )
        result = jnp.dot(
            weights,
            stacked.reshape(9 * channels, block_rows * width),
            preferred_element_type=jnp.float32,
            precision=accuracy,
        )
        result = (result + bias[:, None]).reshape(outputs, block_rows, width)
        result = jnp.maximum(result, 0.0)
        if use_pool:
            result = jnp.max(
                result.reshape(outputs, block_rows // 2, 2, width // 2, 2), axis=(2, 4)
            )
        return result

    blocks = lax.map(one_block, jnp.arange(height // block_rows, dtype=jnp.int32))
    return jnp.transpose(blocks, (1, 0, 2, 3)).reshape(outputs, -1, blocks.shape[-1])


def weight_matrix(weight):
    return jnp.transpose(weight, (2, 0, 1, 3)).reshape(weight.shape[2], -1)


def body(
    query_feats,
    ref_feats,
    pair_table,
    lengths,
    query_len,
    conv1_weight,
    conv1_bias,
    conv2_weight,
    conv2_bias,
    conv3_weight,
    conv3_bias,
    conv4_weight,
    conv4_bias,
):
    qry_index = lax.axis_index("qry")
    ref_index = lax.axis_index("ref")
    frames = query_feats.shape[0]
    regions = query_feats.shape[1]
    channels = query_feats.shape[2]
    tiles_here = pair_table.shape[1] // lax.axis_size("ref")
    tile_rows = ref_feats.shape[0] // tiles_here
    query_mat = query_feats.reshape(frames * regions, channels)
    own_mask = lax.dynamic_slice(pair_table, (qry_index, ref_index * tiles_here), (1, tiles_here))[
        0
    ]
    chosen, picked = slot_table(own_mask, MOST)
    shards = lax.all_gather(ref_feats, "qry", axis=1, tiled=True)
    senders = shards.shape[1]
    sims = frame_sims(query_mat, shards.reshape(tile_rows * senders * regions, channels), regions)
    sims = sims.reshape(1, frames, tile_rows, senders)
    tile_sims = sims.reshape(MOST, frames, frames)
    placed = jnp.einsum(
        "st,sqf->qtf", chosen.astype(jnp.float32), tile_sims, precision=lax.Precision.HIGHEST
    )
    sim_map = placed.reshape(frames, tiles_here * frames)
    padded = padded_2(sim_map, (("qry", 0), ("ref", 1)), 1)
    first_weights = jnp.transpose(conv1_weight, (2, 0, 1)).reshape(conv1_weight.shape[2], 9)
    first = conv_layer(padded[None], first_weights, conv1_bias, 32, True).astype(jnp.bfloat16)
    padded = padded_2(first, (("qry", 1), ("ref", 2)), 1)
    second = conv_layer(padded, weight_matrix(conv2_weight), conv2_bias, 16, True).astype(
        jnp.bfloat16
    )
    padded = padded_2(second, (("qry", 1), ("ref", 2)), 1)
    third = conv_layer(padded, weight_matrix(conv3_weight), conv3_bias, 16, False).astype(
        jnp.bfloat16
    )
    map_rows = third.shape[1]
    map_cols = third.shape[2]
    score_map = (
        jnp.dot(
            conv4_weight[None],
            third.reshape(third.shape[0], -1),
            preferred_element_type=jnp.float32,
        ).reshape(map_rows, map_cols)
        + conv4_bias[0]
    )
    ends = jnp.cumsum(lengths)
    starts = ends - lengths
    column = ref_index * map_cols + jnp.arange(map_cols, dtype=jnp.int32)
    member = (column[:, None] >= starts[None, :]) & (column[:, None] < ends[None, :])
    peaks = jnp.max(jnp.where(member[None], score_map[:, :, None], -jnp.inf), axis=1)
    peaks = lax.pmax(peaks, "ref")
    row_ids = qry_index * map_rows + jnp.arange(map_rows, dtype=jnp.int32)
    partial_value = jnp.sum(jnp.where((row_ids < query_len[0])[:, None], peaks, 0.0), axis=0)
    totals = lax.psum(partial_value, "qry")
    return (score_map, totals / query_len[0].astype(jnp.float32))


def solution(mesh):
    placed = (
        P(("groups", "qry"), None, None),
        P(("groups", "ref"), "qry", None, None),
        P("groups", None),
        P("groups"),
        P("groups"),
        P(),
        P(),
        P(),
        P(),
        P(),
        P(),
        P(),
        P(),
    )
    return jax.shard_map(
        body,
        mesh=mesh,
        in_specs=placed,
        out_specs=(P(("groups", "qry"), "ref"), P("groups")),
        check_vma=False,
    )
```

profile of v0, /device:TPU:0, one launch (start us, length us, event | category | flops | bytes accessed | tf_op | source)
XLA Modules:
  0.0 248.4 jit_solution(3101193552977106752)
XLA Ops:
  7.2 0.7 all-gather.2.cloned.1.call-update
  7.9 1.3 dynamic_slice.23
  10.5 62.7 %all-gather.2.cloned.1.call-done = bf16[32,4,9,3840]{3,0,2,1:T(8,128)(2,1)} async-done(((bf16[32,1,9,3840]{3,0,2,1:T(8,128)(2,1)}), bf16[32,4,9,3840]{3,0,2,1:T(8,128)(2,1)}) %all-gather.2.cloned.1.call-update) | async-done | bytes 8847376 | tf_op jit(solution)/shard_map/all_gather | solution.py:110
  73.2 8.6 %copy.62 = bf16[32,4,9,3840]{3,1,0,2:T(4,128)(2,1)} copy(bf16[32,4,9,3840]{3,0,2,1:T(8,128)(2,1)} %all-gather.2.cloned.1.call-done) | data formatting | bytes 17694720 | tf_op jit(solution)/shard_map/all_gather | solution.py:110
  81.8 12.7 %reshape.195 = bf16[128,9,3840,1]{2,0,1,3:T(8,128)(2,1)} reshape(bf16[32,4,9,3840]{3,1,0,2:T(4,128)(2,1)} %copy.62) | data formatting | bytes 17694720 | tf_op jit(solution)/shard_map/dot_general | solution.py:34
  94.5 18.8 %fusion.7 = f32[128,9,128]{2,0,1:T(8,128)S(1)} fusion(bf16[128,9,3840,1]{2,0,1,3:T(8,128)(2,1)} %reshape.195, bf16[128,9,3840]{2,0,1:T(8,128)(2,1)} %param.19), kind=kOutput, calls=%fused_computation.40 | convolution fusion | flops 10193338368 | bytes 18284544 | tf_op jit(solution)/shard_map/dot_general | solution.py:34
  113.4 2.2 collective-permute-start
  115.6 1.3 collective-permute-start.1
  116.9 1.7 collective-permute-done.1
  118.7 3.4 %collective-permute-start.2 = (f32[130,1]{1,0:T(8,128)S(1)}, f32[130,1]{1,0:T(8,128)S(1)}, u32[]{:S(2)}, u32[]{:S(2)}) collective-permute-start(f32[130,1]{1,0:T(8,128)S(1)} %get-tuple-element.223), channel_id=1, source_target_pairs={{0,1},{1,2},{2,3},{4,5},{5,6},{6,7},{8,9},{9,10},{10,11},{12,13},{... | collective-permute-start | bytes 1568 | tf_op jit(solution)/shard_map/ppermute | solution.py:16
  122.1 1.3 collective-permute-start.3
  124.1 4.3 %collective-permute-done.3 = f32[130,1]{1,0:T(8,128)S(1)} collective-permute-done((f32[130,1]{1,0:T(8,128)S(1)}, f32[130,1]{1,0:T(8,128)S(1)}, u32[]{:S(2)}, u32[]{:S(2)}) %collective-permute-start.3) | collective-permute-done | bytes 552 | tf_op jit(solution)/shard_map/ppermute | solution.py:19
  128.5 23.2 %while.30 = (s32[]{:T(128)}, bf16[4,32,16,64]{3,2,0,1:T(8,128)(2,1)S(1)}, s32[4]{0:T(128)S(1)}, f32[1,130,130]{2,1,0:T(8,128)S(1)}, f32[32,9]{0,1:T(8,128)S(1)},...) while((s32[]{:T(128)}, ...), condition=%wide.region_4.5_spmd, body=%wide.region_2.4_spmd.sunk | while | flops 14647306 | bytes 2885173 | solution.py:75
  128.5 0.6 dynamic_slice.27
  130.5 0.6 fusion.36
  131.6 2.5 %reduce_max.42 = bf16[32,16,64]{0,2,1:T(8,128)(2,1)S(1)} reduce(bf16[32,16,2,64,2]{0,4,3,2,1:T(2,128)(2,1)S(1)} %bitcast.115, bf16[]{:T(256)} %constant.179..sunk), dimensions={2,4}, to_apply=%region_3.3 | reduce | flops 98304 | bytes 327682 | tf_op jit(solution)/shard_map/while/body/eval_jaxpr/reduce_max | solution.py:70
  134.3 0.6 dynamic_slice.27
  136.3 0.6 fusion.36
  137.4 2.5 %reduce_max.42 = bf16[32,16,64]{0,2,1:T(8,128)(2,1)S(1)} reduce(bf16[32,16,2,64,2]{0,4,3,2,1:T(2,128)(2,1)S(1)} %bitcast.115, bf16[]{:T(256)} %constant.179..sunk), dimensions={2,4}, to_apply=%region_3.3 | reduce | flops 98304 | bytes 327682 | tf_op jit(solution)/shard_map/while/body/eval_jaxpr/reduce_max | solution.py:70
  140.1 0.6 dynamic_slice.27
  142.1 0.6 fusion.36
  143.2 2.5 %reduce_max.42 = bf16[32,16,64]{0,2,1:T(8,128)(2,1)S(1)} reduce(bf16[32,16,2,64,2]{0,4,3,2,1:T(2,128)(2,1)S(1)} %bitcast.115, bf16[]{:T(256)} %constant.179..sunk), dimensions={2,4}, to_apply=%region_3.3 | reduce | flops 98304 | bytes 327682 | tf_op jit(solution)/shard_map/while/body/eval_jaxpr/reduce_max | solution.py:70
  145.9 0.6 dynamic_slice.27
  147.9 0.6 fusion.36
  149.0 2.5 %reduce_max.42 = bf16[32,16,64]{0,2,1:T(8,128)(2,1)S(1)} reduce(bf16[32,16,2,64,2]{0,4,3,2,1:T(2,128)(2,1)S(1)} %bitcast.115, bf16[]{:T(256)} %constant.179..sunk), dimensions={2,4}, to_apply=%region_3.3 | reduce | flops 98304 | bytes 327682 | tf_op jit(solution)/shard_map/while/body/eval_jaxpr/reduce_max | solution.py:70
  151.7 2.7 %collective-permute-start.4 = (bf16[32,1,64]{2,1,0:T(2,128)(2,1)S(1)}, bf16[32,1,64]{2,1,0:T(2,128)(2,1)S(1)}, u32[]{:S(2)}, u32[]{:S(2)}) collective-permute-start(bf16[32,1,64]{2,1,0:T(2,128)(2,1)S(1)} %get-tuple-element.217), channel_id=1, source_target_pairs={{0,4},{4,8},{8,12},{1,5},{5,9},{9,13},{2,6},{6,10},{10,14},{3,7},{... | collective-permute-start | bytes 12296 | tf_op jit(solution)/shard_map/ppermute | solution.py:16
  154.5 1.3 collective-permute-start.5
  155.8 2.7 %collective-permute-done.5 = bf16[32,1,64]{2,1,0:T(2,128)(2,1)S(1)} collective-permute-done((bf16[32,1,64]{2,1,0:T(2,128)(2,1)S(1)}, bf16[32,1,64]{2,1,0:T(2,128)(2,1)S(1)}, u32[]{:S(2)}, u32[]{:S(2)}) %collective-permute-start.5) | collective-permute-done | bytes 4128 | tf_op jit(solution)/shard_map/ppermute | solution.py:19
  159.3 3.4 %collective-permute-start.6 = (bf16[32,66,1]{1,0,2:T(8,128)(2,1)S(1)}, bf16[32,66,1]{1,0,2:T(8,128)(2,1)S(1)}, u32[]{:S(2)}, u32[]{:S(2)}) collective-permute-start(bf16[32,66,1]{1,0,2:T(8,128)(2,1)S(1)} %copy.64), channel_id=1, source_target_pairs={{0,1},{1,2},{2,3},{4,5},{5,6},{6,7},{8,9},{9,10},{10,11},{12,13},{... | collective-permute-start | bytes 12680 | tf_op jit(solution)/shard_map/ppermute | solution.py:16
  163.1 1.5 collective-permute-start.7
  164.8 0.9 copy.66
  165.7 2.9 %collective-permute-done.7 = bf16[32,66,1]{1,0,2:T(8,128)(2,1)S(1)} collective-permute-done((bf16[32,66,1]{1,0,2:T(8,128)(2,1)S(1)}, bf16[32,66,1]{1,0,2:T(8,128)(2,1)S(1)}, u32[]{:S(2)}, u32[]{:S(2)}) %collective-permute-start.7) | collective-permute-done | bytes 4256 | tf_op jit(solution)/shard_map/ppermute | solution.py:19
  168.6 0.9 copy.68
  170.1 32.3 %while.31 = (s32[]{:T(128)}, bf16[4,64,8,32]{1,3,2,0:T(8,128)(2,1)}, s32[4]{0:T(128)S(1)}, bf16[32,66,66]{2,0,1:T(8,128)(2,1)S(1)}, bf16[64,288]{1,0:T(8,128)(2,...) while((s32[]{:T(128)}, ...), condition=%wide.region_7.8_spmd, body=%wide.region_5.7_spmd.sunk | while | flops 37994504 | bytes 4822013 | solution.py:75
  170.1 0.6 dynamic_slice.28
  173.1 0.8 copy.113
  174.0 2.4 concatenate.35
  177.0 0.6 reduce_max.43
  177.6 0.6 bitcast_dynamic-update-slice_fusion.2
  181.2 0.8 copy.113
  182.1 2.4 concatenate.35
  185.0 0.6 reduce_max.43
  185.6 0.6 bitcast_dynamic-update-slice_fusion.2
  189.3 0.8 copy.113
  190.1 2.4 concatenate.35
  193.1 0.6 reduce_max.43
  193.7 0.6 bitcast_dynamic-update-slice_fusion.2
  197.4 0.8 copy.113
  198.2 2.4 concatenate.35
  201.2 0.6 reduce_max.43
  201.8 0.6 bitcast_dynamic-update-slice_fusion.2
  202.4 0.7 fusion.14
  203.1 2.9 %collective-permute-start.8 = (bf16[64,1,32]{0,2,1:T(8,128)(2,1)S(1)}, bf16[64,1,32]{0,2,1:T(8,128)(2,1)S(1)}, u32[]{:S(2)}, u32[]{:S(2)}) collective-permute-start(bf16[64,1,32]{0,2,1:T(8,128)(2,1)S(1)} %get-tuple-element.221), channel_id=1, source_target_pairs={{0,4},{4,8},{8,12},{1,5},{5,9},{9,13},{2,6},{6,10},{10,14},{3,7},{... | collective-permute-start | bytes 12296 | tf_op jit(solution)/shard_map/ppermute | solution.py:16
  206.1 1.3 collective-permute-start.9
  208.1 2.0 collective-permute-done.9
  210.1 0.9 pad_maximum_fusion.6
  211.0 3.4 %collective-permute-start.10 = (bf16[64,34,1]{0,2,1:T(2,128)(2,1)S(1)}, bf16[64,34,1]{0,2,1:T(2,128)(2,1)S(1)}, u32[]{:S(2)}, u32[]{:S(2)}) collective-permute-start(bf16[64,34,1]{0,2,1:T(2,128)(2,1)S(1)} %get-tuple-element.219), channel_id=1, source_target_pairs={{0,1},{1,2},{2,3},{4,5},{5,6},{6,7},{8,9},{9,10},{10,11},{12,13},{... | collective-permute-start | bytes 13064 | tf_op jit(solution)/shard_map/ppermute | solution.py:16
  214.4 1.3 collective-permute-start.11
  215.8 1.1 copy.71
  217.5 2.6 %collective-permute-done.11 = bf16[64,34,1]{0,2,1:T(2,128)(2,1)S(1)} collective-permute-done((bf16[64,34,1]{0,2,1:T(2,128)(2,1)S(1)}, bf16[64,34,1]{0,2,1:T(2,128)(2,1)S(1)}, u32[]{:S(2)}, u32[]{:S(2)}) %collective-permute-start.11) | collective-permute-done | bytes 4384 | tf_op jit(solution)/shard_map/ppermute | solution.py:19
  220.1 1.1 pad_maximum_fusion.2
  221.2 4.8 %while.32 = (s32[]{:T(128)}, bf16[2,128,16,32]{1,3,2,0:T(8,128)(2,1)S(1)}, s32[2]{0:T(128)S(1)}, bf16[64,34,34]{0,2,1:T(8,128)(2,1)S(1)}, bf16[128,576]{1,0:T(8,...) while((s32[]{:T(128)}, ...), condition=%wide.region_9.10_spmd, body=%wide.region_8.9_spmd.sunk | while | flops 75694088 | bytes 3490551 | solution.py:75
  226.6 8.5 %pmax.7 = f32[32,2]{0,1:T(2,128)S(1)} all-reduce(f32[32,2]{0,1:T(2,128)S(1)} %select_reduce_fusion), channel_id=1, replica_groups=mesh['groups'=2,'qry'=4,'ref'=4] {'ref'}, use_global_device_ids=true, to_apply=%region_12.13 | all-reduce | flops 64 | bytes 512 | tf_op jit(solution)/shard_map/pmax | solution.py:145
  235.2 5.8 %psum.7 = f32[2]{0:T(128)S(1)} all-reduce(f32[2]{0:T(128)S(1)} %select_reduce_fusion.1), channel_id=1, replica_groups=mesh['groups'=2,'qry'=4,'ref'=4] {'qry'}, use_global_device_ids=true, to_apply=%region_14.15 | all-reduce | flops 2 | bytes 16 | tf_op jit(solution)/shard_map/psum | solution.py:148
  (167 shorter events, 23.9 us)
Async XLA Ops:
  7.2 218.9 %copy-start = (bf16[128]{0:T(256)(128)(2,1)S(1)}, bf16[128]{0:T(256)(128)(2,1)}, u32[]{:S(2)}) copy-start(bf16[128]{0:T(256)(128)(2,1)} %param.30) | copy-start | bytes 772
  7.2 66.0 %all-gather.2.cloned.1.call-start = ((), (), s32[]{:S(2)}) async-start(), calls=%async_computation | async-start | bytes 11059200 | tf_op jit(solution)/shard_map/all_gather | solution.py:110
  94.5 28.9 %copy-start.6 = (f32[3,3,32]{2,1,0:T(4,128)S(1)}, f32[3,3,32]{2,1,0:T(4,128)}, u32[]{:S(2)}) copy-start(f32[3,3,32]{2,1,0:T(4,128)} %param.24) | copy-start | bytes 3460
  94.5 29.0 %copy-start.7 = (s32[2]{0:T(128)S(1)}, s32[2]{0:T(128)}, u32[]{:S(2)}) copy-start(s32[2]{0:T(128)} %param.22) | copy-start | bytes 28
  94.5 34.0 %copy-start.5 = (f32[32]{0:T(128)S(1)}, f32[32]{0:T(128)}, u32[]{:S(2)}) copy-start(f32[32]{0:T(128)} %param.25) | copy-start | bytes 388
  113.4 3.5 %collective-permute-start = (f32[1,128]{1,0:T(1,128)S(1)}, f32[1,128]{1,0:T(1,128)S(1)}, u32[]{:S(2)}, u32[]{:S(2)}) collective-permute-start(f32[1,128]{1,0:T(1,128)S(1)} %get-tuple-element.225), channel_id=1, source_target_pairs={{0,4},{4,8},{8,12},{1,5},{5,9},{9,13},{2,6},{6,10},{10,14},{3,7},{... | collective-permute-start | bytes 1544 | tf_op jit(solution)/shard_map/ppermute | solution.py:16
  115.6 3.1 %collective-permute-start.1 = (f32[1,128]{1,0:T(1,128)S(1)}, f32[1,128]{1,0:T(1,128)S(1)}, u32[]{:S(2)}, u32[]{:S(2)}) collective-permute-start(f32[1,128]{1,0:T(1,128)S(1)} %get-tuple-element.226), channel_id=1, source_target_pairs={{4,0},{8,4},{12,8},{5,1},{9,5},{13,9},{6,2},{10,6},{14,10},{7,3},{... | collective-permute-start | bytes 1544 | tf_op jit(solution)/shard_map/ppermute | solution.py:19
  118.7 5.3 %collective-permute-start.2 = (f32[130,1]{1,0:T(8,128)S(1)}, f32[130,1]{1,0:T(8,128)S(1)}, u32[]{:S(2)}, u32[]{:S(2)}) collective-permute-start(f32[130,1]{1,0:T(8,128)S(1)} %get-tuple-element.223), channel_id=1, source_target_pairs={{0,1},{1,2},{2,3},{4,5},{5,6},{6,7},{8,9},{9,10},{10,11},{12,13},{... | collective-permute-start | bytes 1568 | tf_op jit(solution)/shard_map/ppermute | solution.py:16
  122.1 6.2 %collective-permute-start.3 = (f32[130,1]{1,0:T(8,128)S(1)}, f32[130,1]{1,0:T(8,128)S(1)}, u32[]{:S(2)}, u32[]{:S(2)}) collective-permute-start(f32[130,1]{1,0:T(8,128)S(1)} %get-tuple-element.224), channel_id=1, source_target_pairs={{1,0},{2,1},{3,2},{5,4},{6,5},{7,6},{9,8},{10,9},{11,10},{13,12},{... | collective-permute-start | bytes 1568 | tf_op jit(solution)/shard_map/ppermute | solution.py:19
  128.5 36.1 %copy-start.1 = (bf16[3,3,64,32]{2,3,1,0:T(8,128)(2,1)S(1)}, bf16[3,3,64,32]{2,3,1,0:T(8,128)(2,1)}, u32[]{:S(2)}) copy-start(bf16[3,3,64,32]{2,3,1,0:T(8,128)(2,1)} %param.26) | copy-start | bytes 110596
  151.7 18.4 %copy-start.3 = (f32[64]{0:T(128)S(1)}, f32[64]{0:T(128)}, u32[]{:S(2)}) copy-start(f32[64]{0:T(128)} %param.27) | copy-start | bytes 772
  151.7 4.1 %collective-permute-start.4 = (bf16[32,1,64]{2,1,0:T(2,128)(2,1)S(1)}, bf16[32,1,64]{2,1,0:T(2,128)(2,1)S(1)}, u32[]{:S(2)}, u32[]{:S(2)}) collective-permute-start(bf16[32,1,64]{2,1,0:T(2,128)(2,1)S(1)} %get-tuple-element.217), channel_id=1, source_target_pairs={{0,4},{4,8},{8,12},{1,5},{5,9},{9,13},{2,6},{6,10},{10,14},{3,7},{... | collective-permute-start | bytes 12296 | tf_op jit(solution)/shard_map/ppermute | solution.py:16
  154.5 4.1 %collective-permute-start.5 = (bf16[32,1,64]{2,1,0:T(2,128)(2,1)S(1)}, bf16[32,1,64]{2,1,0:T(2,128)(2,1)S(1)}, u32[]{:S(2)}, u32[]{:S(2)}) collective-permute-start(bf16[32,1,64]{2,1,0:T(2,128)(2,1)S(1)} %get-tuple-element.218), channel_id=1, source_target_pairs={{4,0},{8,4},{12,8},{5,1},{9,5},{13,9},{6,2},{10,6},{14,10},{7,3},{... | collective-permute-start | bytes 12296 | tf_op jit(solution)/shard_map/ppermute | solution.py:19
  159.3 5.4 %collective-permute-start.6 = (bf16[32,66,1]{1,0,2:T(8,128)(2,1)S(1)}, bf16[32,66,1]{1,0,2:T(8,128)(2,1)S(1)}, u32[]{:S(2)}, u32[]{:S(2)}) collective-permute-start(bf16[32,66,1]{1,0,2:T(8,128)(2,1)S(1)} %copy.64), channel_id=1, source_target_pairs={{0,1},{1,2},{2,3},{4,5},{5,6},{6,7},{8,9},{9,10},{10,11},{12,13},{... | collective-permute-start | bytes 12680 | tf_op jit(solution)/shard_map/ppermute | solution.py:16
  163.1 5.5 %collective-permute-start.7 = (bf16[32,66,1]{1,0,2:T(8,128)(2,1)S(1)}, bf16[32,66,1]{1,0,2:T(8,128)(2,1)S(1)}, u32[]{:S(2)}, u32[]{:S(2)}) collective-permute-start(bf16[32,66,1]{1,0,2:T(8,128)(2,1)S(1)} %copy.65), channel_id=1, source_target_pairs={{1,0},{2,1},{3,2},{5,4},{6,5},{7,6},{9,8},{10,9},{11,10},{13,12},{... | collective-permute-start | bytes 12680 | tf_op jit(solution)/shard_map/ppermute | solution.py:19
  170.1 51.1 %copy-start.4 = (f32[128]{0:T(128)S(1)}, f32[128]{0:T(128)}, u32[]{:S(2)}) copy-start(f32[128]{0:T(128)} %param.29) | copy-start | bytes 1540
  203.1 5.0 %collective-permute-start.8 = (bf16[64,1,32]{0,2,1:T(8,128)(2,1)S(1)}, bf16[64,1,32]{0,2,1:T(8,128)(2,1)S(1)}, u32[]{:S(2)}, u32[]{:S(2)}) collective-permute-start(bf16[64,1,32]{0,2,1:T(8,128)(2,1)S(1)} %get-tuple-element.221), channel_id=1, source_target_pairs={{0,4},{4,8},{8,12},{1,5},{5,9},{9,13},{2,6},{6,10},{10,14},{3,7},{... | collective-permute-start | bytes 12296 | tf_op jit(solution)/shard_map/ppermute | solution.py:16
  206.1 4.0 %collective-permute-start.9 = (bf16[64,1,32]{0,2,1:T(8,128)(2,1)S(1)}, bf16[64,1,32]{0,2,1:T(8,128)(2,1)S(1)}, u32[]{:S(2)}, u32[]{:S(2)}) collective-permute-start(bf16[64,1,32]{0,2,1:T(8,128)(2,1)S(1)} %get-tuple-element.222), channel_id=1, source_target_pairs={{4,0},{8,4},{12,8},{5,1},{9,5},{13,9},{6,2},{10,6},{14,10},{7,3},{... | collective-permute-start | bytes 12296 | tf_op jit(solution)/shard_map/ppermute | solution.py:19
  211.0 6.5 %collective-permute-start.10 = (bf16[64,34,1]{0,2,1:T(2,128)(2,1)S(1)}, bf16[64,34,1]{0,2,1:T(2,128)(2,1)S(1)}, u32[]{:S(2)}, u32[]{:S(2)}) collective-permute-start(bf16[64,34,1]{0,2,1:T(2,128)(2,1)S(1)} %get-tuple-element.219), channel_id=1, source_target_pairs={{0,1},{1,2},{2,3},{4,5},{5,6},{6,7},{8,9},{9,10},{10,11},{12,13},{... | collective-permute-start | bytes 13064 | tf_op jit(solution)/shard_map/ppermute | solution.py:16
  214.4 5.6 %collective-permute-start.11 = (bf16[64,34,1]{0,2,1:T(2,128)(2,1)S(1)}, bf16[64,34,1]{0,2,1:T(2,128)(2,1)S(1)}, u32[]{:S(2)}, u32[]{:S(2)}) collective-permute-start(bf16[64,34,1]{0,2,1:T(2,128)(2,1)S(1)} %get-tuple-element.220), channel_id=1, source_target_pairs={{1,0},{2,1},{3,2},{5,4},{6,5},{7,6},{9,8},{10,9},{11,10},{13,12},{... | collective-permute-start | bytes 13064 | tf_op jit(solution)/shard_map/ppermute | solution.py:19
  226.5 15.1 %copy-start.2 = (f32[32,32]{1,0:T(8,128)}, f32[32,32]{1,0:T(8,128)S(1)}, u32[]{:S(2)}) copy-start(f32[32,32]{1,0:T(8,128)S(1)} %broadcast_add_fusion) | copy-start | bytes 12292
Sparse Core Ops, SparseCore 0:
  9.5 63.5 all-gather.1
where the time goes:
time: 250 us; the launch traced here: 248 us
  waiting for transfers between devices  80 us (32%)
  local copies, waits for them, and re-layouts  63.7 us (25%)
  starting transfers between devices  26 us (10%)
  matrix products  23.9 us (10%)
  between operations  17.1 us (7%)
  other arithmetic  16.3 us (7%)
  blocking collectives  14.3 us (6%)
  loops' own time  7.15 us (3%)
    all_gather x1, waiting for transfers between devices, body(): shards = lax.all_gather(ref_feats, 'qry', axis=1, tiled=True)  62.7 us
    dot_general x1, matrix products, frame_sims(): lax.dot_general(query_mat, ref_mat, (((1,), (1,)), ((), ())), preferred_e...  18.8 us
    ppermute x6, starting transfers between devices, padded_2(): lax.ppermute(lax.slice_in_dim(block, block.shape[dim] - width, None, axis...  18 us
    ppermute x6, waiting for transfers between devices, padded_2(): lax.ppermute(lax.slice_in_dim(block, 0, width, axis=dim), axis, backward)  16.2 us
    dot_general x1, local copies, waits for them, and re-layouts, frame_sims(): lax.dot_general(query_mat, ref_mat, (((1,), (1,)), ((), ())), preferred_e...  12.7 us
    reduce_max x8, other arithmetic, one_block(): jnp.max(result.reshape(outputs, block_rows // 2, 2, width // 2, 2), axis=...  12.3 us
    while x76, local copies, waits for them, and re-layouts  11.5 us
    concatenate x10, local copies, waits for them, and re-layouts, one_block(): jnp.concatenate([window[:, shift_row:shift_row + block_rows, shift_col:sh...  11 us
  transfers between devices with their start and end apart: 13, of which 8 were waited for; matrix products, arithmetic and copies ran while one was open for 2% of the time, Pallas kernels for 0%

commit v1 on v0

v1 whole, which is shorter than its diff:
```python
import functools
import math

import jax
import jax.numpy as jnp
import numpy as np
from jax import lax
from jax.experimental import pallas as pl
from jax.experimental.pallas import tpu as pltpu
from jax.sharding import PartitionSpec as P

MESH = pl.DeviceIdType.MESH
HALO = 8
PITCH = 40
LEAD = 48


def sims_kernel(
    chips, regions, frames, scale, chunk, q_hbm, r_hbm, out_ref, q_buf, r_buf, acc,
    q_sem, own_sem, send_x, recv_x, send_s, recv_s,
):
    depth = r_hbm.shape[1]
    steps = depth // chunk
    shard = r_hbm.shape[0] // regions
    parts = regions * frames // 384
    me = lax.axis_index("qry")
    chip = me // 2
    core = me % 2
    sibling = chip * 2 + (1 - core)
    right = ((chip + 1) % chips) * 2 + core
    left = ((chip + chips - 1) % chips) * 2 + core

    def cols(c):
        return pl.ds(pl.multiple_of(c * chunk, 128), chunk)

    def own_copy(c):
        return pltpu.make_async_copy(
            r_hbm.at[:, cols(c)], r_buf.at[0, :, cols(c)], own_sem.at[c]
        )

    def q_copy(c):
        return pltpu.make_async_copy(q_hbm.at[:, cols(c)], q_buf.at[:, cols(c)], q_sem.at[c])

    def to_right(step, c):
        source = r_hbm if step == 0 else r_buf.at[2 * step]
        return pltpu.make_async_remote_copy(
            src_ref=source.at[:, cols(c)],
            dst_ref=r_buf.at[2 * step + 2, :, cols(c)],
            send_sem=send_x.at[step, c],
            recv_sem=recv_x.at[step, c],
            device_id={"qry": right},
            device_id_type=MESH,
        )

    def to_sibling(step, c):
        source = r_hbm if step == 0 else r_buf.at[2 * step]
        return pltpu.make_async_remote_copy(
            src_ref=source.at[:, cols(c)],
            dst_ref=r_buf.at[2 * step + 1, :, cols(c)],
            send_sem=send_s.at[step, c],
            recv_sem=recv_s.at[step, c],
            device_id={"qry": sibling},
            device_id_type=MESH,
        )

    def start_own(c, carry):
        own_copy(c).start()
        q_copy(c).start()
        return carry

    lax.fori_loop(0, steps, start_own, 0)
    barrier = pltpu.get_barrier_semaphore()
    greet = (sibling, right) if chips == 2 else (sibling, right, left)
    for device in greet:
        pl.semaphore_signal(barrier, inc=1, device_id={"qry": device}, device_id_type=MESH)
    pl.semaphore_wait(barrier, len(greet))

    def start_sends(c, carry):
        to_right(0, c).start()
        to_sibling(0, c).start()
        return carry

    lax.fori_loop(0, steps, start_sends, 0)

    def multiply(slot, side, c):
        block = r_buf[slot, :, cols(c)]

        def one_part(i, carry):
            rows = pl.ds(pl.multiple_of(i * 384, 128), 384)
            term = lax.dot_general(
                block, q_buf[rows, cols(c)], (((1,), (1,)), ((), ())),
                preferred_element_type=jnp.float32,
            )
            kept = acc[side, i]
            acc[side, i] = jnp.where(c == 0, term, kept + term)
            return carry

        lax.fori_loop(0, parts, one_part, 0)

    def finish(step, side):
        origin = (chip + chips - step) % chips
        source = origin * 2 + (core if side == 0 else 1 - core)
        total = jnp.zeros((shard, frames), jnp.float32)
        for i in range(parts):
            best = jnp.max(acc[side, i].reshape(regions, shard, 384), axis=0)
            for k in range(384 // frames):
                total = total + best[:, k * frames : (k + 1) * frames]
        out_ref[source] = total * scale

    acc[...] = jnp.zeros_like(acc)

    def first_own(c, carry):
        own_copy(c).wait()
        q_copy(c).wait()
        multiply(0, 0, c)
        return carry

    lax.fori_loop(0, steps, first_own, 0)
    finish(0, 0)

    def first_sibling(c, carry):
        to_sibling(0, c).wait_recv()
        multiply(1, 1, c)
        return carry

    lax.fori_loop(0, steps, first_sibling, 0)
    finish(0, 1)
    for step in range(1, chips):

        def later(c, carry):
            to_right(step - 1, c).wait_recv()
            to_sibling(step, c).start()
            if step < chips - 1:
                to_right(step, c).start()
            multiply(2 * step, 0, c)
            to_sibling(step, c).wait_recv()
            multiply(2 * step + 1, 1, c)
            return carry

        lax.fori_loop(0, steps, later, 0)
        finish(step, 0)
        finish(step, 1)

    def drain(c, carry):
        for step in range(chips):
            to_sibling(step, c).wait_send()
            if step < chips - 1:
                to_right(step, c).wait_send()
        return carry

    lax.fori_loop(0, steps, drain, 0)


def frame_sims(query_mat, ref_mat, regions, senders):
    depth = query_mat.shape[1]
    frames = query_mat.shape[0] // regions
    rows = ref_mat.shape[0]
    shard = rows // regions
    chips = senders // 2
    chunk = 768 if depth % 768 == 0 else depth
    steps = depth // chunk
    parts = regions * frames // 384
    scale = 1.0 / (regions * math.sqrt(depth))
    return pl.pallas_call(
        functools.partial(sims_kernel, chips, regions, frames, scale, chunk),
        out_shape=jax.ShapeDtypeStruct((senders, shard, frames), jnp.float32),
        in_specs=[pl.BlockSpec(memory_space=pl.ANY)] * 2,
        out_specs=pl.BlockSpec(memory_space=pltpu.VMEM),
        scratch_shapes=[
            pltpu.VMEM(query_mat.shape, jnp.bfloat16),
            pltpu.VMEM((senders, rows, depth), jnp.bfloat16),
            pltpu.VMEM((2, parts, rows, 384), jnp.float32),
            pltpu.SemaphoreType.DMA((steps,)),
            pltpu.SemaphoreType.DMA((steps,)),
            pltpu.SemaphoreType.DMA((chips, steps)),
            pltpu.SemaphoreType.DMA((chips, steps)),
            pltpu.SemaphoreType.DMA((chips, steps)),
            pltpu.SemaphoreType.DMA((chips, steps)),
        ],
        compiler_params=pltpu.CompilerParams(
            collective_id=0, has_side_effects=True, vmem_limit_bytes=48 << 20
        ),
        name="frame_sims",
    )(query_mat, ref_mat)


def net_kernel(
    tiles_p, tiles_f, where_ref, map_ref, w1_ref, b1_ref, w2_ref, b2_ref, w3_ref, b3_ref,
    w4_ref, out_ref, z_buf, x_buf, first_buf, second_buf, w2_full, w3_full,
):
    side = tiles_p + 4
    rows = side * PITCH
    wide = map_ref.shape[0]
    lane = lax.broadcasted_iota(jnp.int32, (1, 128), 1)
    low_a = lane < 64
    low_b = (lane % 64) < 32

    w2_full[...] = jnp.zeros_like(w2_full)
    taps = {(0, 0): 0, (0, 1): 1, (1, 0): 2, (1, 1): -1}
    for g in range(2):
        for h in range(2):
            for a in range(2):
                for b in range(2):
                    row = ((g * 2 + h) * 4 + a * 2 + b) * 32
                    for u in range(2):
                        for v in range(2):
                            di = taps[g, a] - u + 1
                            dj = taps[h, b] - v + 1
                            if 0 <= di < 3 and 0 <= dj < 3:
                                col = u * 128 + v * 64
                                w2_full[row : row + 32, col : col + 64] = w2_ref[di * 3 + dj]
    for k in range(9):
        w3_full[k * 64 : (k + 1) * 64, :] = w3_ref[k]
    w3_full[576:640, :] = jnp.zeros((64, 128), jnp.bfloat16)

    source = lax.broadcasted_iota(jnp.int32, (wide, 128), 0)
    target = lax.broadcasted_iota(jnp.int32, (wide, 128), 1)
    whole = map_ref[...]
    high = whole.astype(jnp.bfloat16)
    lower = (whole - high.astype(jnp.float32)).astype(jnp.bfloat16)
    z_buf[...] = jnp.zeros_like(z_buf)
    for rr in range(6):
        pick = jnp.where(source == 4 * target - 1 + rr, 1.0, 0.0).astype(jnp.bfloat16)
        for part, value in enumerate((high, lower)):
            z_buf[part, 8 : 8 + wide, rr * 128 : (rr + 1) * 128] = jnp.dot(
                value, pick, preferred_element_type=jnp.float32
            )
    for block in range(side):
        pieces = []
        for part in (0, 1, 0):
            for rr in range(6):
                pieces.append(
                    z_buf[part, 4 * block + 7 : 4 * block + 15, rr * 128 : (rr + 1) * 128]
                )
        flat = jnp.concatenate(pieces, axis=0)
        x_buf[block * PITCH : (block + 1) * PITCH, :] = jnp.transpose(flat)[:PITCH]

    shape = (side, PITCH, 128)
    at_f = lax.broadcasted_iota(jnp.int32, shape, 0) + (where_ref[1] - 2)
    at_p = lax.broadcasted_iota(jnp.int32, shape, 1) + (where_ref[0] - 2)
    inside = (at_f >= 0) & (at_f < where_ref[3]) & (at_p >= 0) & (at_p < where_ref[2])
    inside = jnp.where(inside, 1.0, 0.0).reshape(rows, 128)

    made = jnp.dot(
        x_buf[...].astype(jnp.bfloat16), w1_ref[...], preferred_element_type=jnp.float32
    )
    best = jnp.maximum(
        jnp.maximum(made[:, 0:128], made[:, 128:256]),
        jnp.maximum(made[:, 256:384], made[:, 384:512]),
    )
    first = jnp.maximum(best + b1_ref[...], 0.0)
    first = jnp.where(inside > 0.5, first, 0.0).astype(jnp.bfloat16).astype(jnp.float32)
    first_buf[0:LEAD, :] = jnp.zeros((LEAD, 128), jnp.float32)
    first_buf[LEAD + rows :, :] = jnp.zeros((LEAD, 128), jnp.float32)
    first_buf[LEAD : LEAD + rows, :] = first

    start = LEAD - PITCH
    more = rows + 2 * PITCH
    shifted = jnp.where(
        low_a, first_buf[start + 1 : start + 1 + more, :], first_buf[start - 1 : start - 1 + more, :]
    )
    across = jnp.where(
        low_b, first_buf[LEAD + PITCH : LEAD + PITCH + rows, :], first_buf[start : start + rows, :]
    )
    both = jnp.where(low_b, shifted[2 * PITCH :], shifted[:rows])
    stacked = jnp.concatenate(
        [first, across, shifted[PITCH : PITCH + rows], both], axis=1
    ).astype(jnp.bfloat16)
    made = jnp.dot(stacked, w2_full[...], preferred_element_type=jnp.float32)
    best = jnp.maximum(made[:, 0:128], made[:, 128:256])
    best = jnp.maximum(best, pltpu.roll(best, 64, 1))
    second = jnp.maximum(best + b2_ref[...], 0.0)
    second = jnp.where(inside > 0.5, second, 0.0).astype(jnp.bfloat16).astype(jnp.float32)
    second_buf[0:LEAD, :] = jnp.zeros((LEAD, 128), jnp.float32)
    second_buf[LEAD + rows :, :] = jnp.zeros((LEAD, 128), jnp.float32)
    second_buf[LEAD : LEAD + rows, :] = second

    def moved(k):
        di, dj = k // 3, k % 3
        begin = LEAD + (dj - 1) * PITCH + di - 1
        return second_buf[begin : begin + rows, :]

    groups = []
    for k in range(0, 9, 2):
        groups.append(jnp.where(low_a, moved(k), moved(k + 1)) if k < 8 else moved(k))
    stacked = jnp.concatenate(groups, axis=1).astype(jnp.bfloat16)
    made = jnp.dot(stacked, w3_full[...], preferred_element_type=jnp.float32)
    third = jnp.maximum(made + b3_ref[...], 0.0).astype(jnp.bfloat16).astype(jnp.float32)
    weighted = third * w4_ref[...]
    out_ref[...] = jnp.sum(weighted.reshape(side, PITCH, 128), axis=2)


def first_matrix(weight):
    outputs = weight.shape[2]
    table = np.zeros((6, 8, 2, 2, 2, 2, 9), np.float32)
    for a in range(2):
        for b in range(2):
            for u in range(2):
                for v in range(2):
                    for di in range(3):
                        for dj in range(3):
                            table[2 * a + u + di, 2 * b + v + dj, u, v, a, b, di * 3 + dj] = 1.0
    full = jnp.dot(
        table.reshape(48 * 16, 9), weight.reshape(9, outputs), precision=lax.Precision.HIGHEST
    ).reshape(48, 16 * outputs)
    high = lax.reduce_precision(full, 8, 7)
    return jnp.concatenate([high, high, full - high], axis=0).astype(jnp.bfloat16)


def network(
    wide_map, where, tiles, w1, b1, w2, b2, w3, b3, w4
):
    side = tiles + 4
    rows = side * PITCH
    vmem = pl.BlockSpec(memory_space=pltpu.VMEM)
    return pl.pallas_call(
        functools.partial(net_kernel, tiles, tiles),
        out_shape=jax.ShapeDtypeStruct((side, PITCH), jnp.float32),
        in_specs=[pl.BlockSpec(memory_space=pltpu.SMEM)] + [vmem] * 8,
        out_specs=vmem,
        scratch_shapes=[
            pltpu.VMEM((2, wide_map.shape[0] + 16, 768), jnp.float32),
            pltpu.VMEM((rows, 144), jnp.float32),
            pltpu.VMEM((rows + 2 * LEAD, 128), jnp.float32),
            pltpu.VMEM((rows + 2 * LEAD, 128), jnp.float32),
            pltpu.VMEM((512, 256), jnp.bfloat16),
            pltpu.VMEM((640, 128), jnp.bfloat16),
        ],
        compiler_params=pltpu.CompilerParams(vmem_limit_bytes=48 << 20),
        name="network",
    )(
        where,
        wide_map,
        w1,
        jnp.tile(b1, 4)[None],
        jnp.transpose(w2, (0, 1, 3, 2)).reshape(9, w2.shape[3], w2.shape[2]),
        jnp.tile(b2, 2)[None],
        jnp.transpose(w3, (0, 1, 3, 2)).reshape(9, w3.shape[3], w3.shape[2]),
        b3[None],
        w4.astype(jnp.float32)[None],
    )


def padded(block, sides, width):
    for axis, dim in sides:
        count = lax.axis_size(axis)
        forward = [(i, i + 1) for i in range(count - 1)]
        backward = [(target, source) for source, target in forward]
        low = lax.ppermute(
            lax.slice_in_dim(block, block.shape[dim] - width, None, axis=dim), axis, forward
        )
        high = lax.ppermute(lax.slice_in_dim(block, 0, width, axis=dim), axis, backward)
        block = jnp.concatenate([low, block, high], axis=dim)
    return block


def body(
    query_feats, ref_feats, pair_table, lengths, query_len, conv1_weight, conv1_bias,
    conv2_weight, conv2_bias, conv3_weight, conv3_bias, conv4_weight, conv4_bias,
):
    qry_index = lax.axis_index("qry")
    ref_index = lax.axis_index("ref")
    senders = lax.axis_size("qry")
    frames, regions, channels = query_feats.shape
    query_mat = jnp.transpose(query_feats, (1, 0, 2)).reshape(regions * frames, channels)
    ref_mat = jnp.transpose(ref_feats, (1, 2, 0, 3)).reshape(-1, channels)
    sims = frame_sims(query_mat, ref_mat, regions, senders)
    active = lax.dynamic_slice(pair_table, (qry_index, ref_index), (1, 1)) == 1
    sims = jnp.transpose(sims, (1, 0, 2)).reshape(frames, frames)
    sims = jnp.where(active, sims, 0.0)
    wide_map = padded(sims, (("ref", 0), ("qry", 1)), HALO)
    tiles = frames // 4
    where = jnp.stack(
        [
            qry_index * tiles,
            ref_index * tiles,
            jnp.int32(senders * tiles),
            jnp.int32(lax.axis_size("ref") * tiles),
        ]
    ).astype(jnp.int32)
    scores = network(
        wide_map, where, tiles, first_matrix(conv1_weight), conv1_bias, conv2_weight,
        conv2_bias, conv3_weight, conv3_bias, conv4_weight,
    )
    score_map = jnp.transpose(scores[2 : 2 + tiles, 2 : 2 + tiles]) + conv4_bias[0]
    ends = jnp.cumsum(lengths)
    starts = ends - lengths
    column = ref_index * tiles + jnp.arange(tiles, dtype=jnp.int32)
    member = (column[:, None] >= starts[None, :]) & (column[:, None] < ends[None, :])
    peaks = jnp.max(jnp.where(member[None], score_map[:, :, None], -jnp.inf), axis=1)
    peaks = lax.pmax(peaks, "ref")
    row_ids = qry_index * tiles + jnp.arange(tiles, dtype=jnp.int32)
    partial_value = jnp.sum(jnp.where((row_ids < query_len[0])[:, None], peaks, 0.0), axis=0)
    totals = lax.psum(partial_value, "qry")
    return (score_map, totals / query_len[0].astype(jnp.float32))


def solution(mesh):
    placed = (
        P(("groups", "qry"), None, None),
        P(("groups", "ref"), "qry", None, None),
        P("groups", None),
        P("groups"),
        P("groups"),
    ) + (P(),) * 8
    return jax.shard_map(
        body,
        mesh=mesh,
        in_specs=placed,
        out_specs=(P(("groups", "qry"), "ref"), P("groups")),
        check_vma=False,
    )
```

time: 250 us -> 96.6 us (0.39)
  waiting for transfers between devices: 80 us -> 4.71 us
  local copies, waits for them, and re-layouts: 63.7 us -> 3.53 us
  Pallas kernels: 0 us -> 58.8 us
  matrix products: 23.9 us -> 0.44 us
  starting transfers between devices: 26 us -> 7.35 us
  other arithmetic: 16.3 us -> 1.32 us
  between operations: 17.1 us -> 2.88 us
  loops' own time: 7.15 us -> 0 us
  blocking collectives: 14.3 us -> 17.2 us
    all_gather x1 -> x0, waiting for transfers between devices: 62.7 us -> none  [body(): shards = lax.all_gather(ref_feats, 'qry', axis=1, tiled=True)]
    pallas_call x0 -> x2, Pallas kernels: none -> 58.8 us  [the longest x1 55.1 us: frame_sims(): pl.pallas_call(functools.partial(sims_kernel, chips, regions, frames, sca...]
    dot_general x12 -> x1, matrix products: 23.9 us -> 0.44 us  [first_matrix(): jnp.dot(table.reshape(48 * 16, 9), weight.reshape(9, outputs), precision=...]
    ppermute x12 -> x4, starting transfers between devices: 26 us -> 7.35 us  [the longest x2 4.76 us: padded(): lax.ppermute(lax.slice_in_dim(block, block.shape[dim] - width, None, axis...]
    dot_general x1 -> x0, local copies, waits for them, and re-layouts: 12.7 us -> none  [frame_sims(): lax.dot_general(query_mat, ref_mat, (((1,), (1,)), ((), ())), preferred_e...]
    while x78 -> x0, local copies, waits for them, and re-layouts: 12.7 us -> none
    reduce_max x8 -> x0, other arithmetic: 12.3 us -> none  [one_block(): jnp.max(result.reshape(outputs, block_rows // 2, 2, width // 2, 2), axis=...]
    ppermute x12 -> x4, waiting for transfers between devices: 16.6 us -> 4.71 us  [the longest x2 4.7 us: padded(): lax.ppermute(lax.slice_in_dim(block, 0, width, axis=dim), axis, backward)]
  transfers between devices with their start and end apart: 13 -> 4, of which waited for: 8 -> 2; matrix products, arithmetic and copies ran while one was open for 2% -> 1% of each run, Pallas kernels for 0% -> 0%
where the time goes in v1:
time: 96.6 us; the launch traced here: 96.3 us
  Pallas kernels  58.8 us (61%)
  blocking collectives  17.2 us (18%)
  starting transfers between devices  7.35 us (8%)
  waiting for transfers between devices  4.71 us (5%)
  local copies, waits for them, and re-layouts  3.53 us (4%)
  between operations  2.88 us (3%)
  other arithmetic  1.32 us (1%)
    pallas_call x1, Pallas kernels, frame_sims(): pl.pallas_call(functools.partial(sims_kernel, chips, regions, frames, sca...  55.1 us
    pmax x1, blocking collectives, body(): peaks = lax.pmax(peaks, 'ref')  10.6 us
    psum x1, blocking collectives, body(): totals = lax.psum(partial_value, 'qry')  6.64 us
    ppermute x2, starting transfers between devices, padded(): lax.ppermute(lax.slice_in_dim(block, block.shape[dim] - width, None, axis...  4.76 us
    ppermute x2, waiting for transfers between devices, padded(): lax.ppermute(lax.slice_in_dim(block, 0, width, axis=dim), axis, backward)  4.7 us
    pallas_call x1, Pallas kernels, network(): pl.pallas_call(functools.partial(net_kernel, tiles, tiles), out_shape=jax...  3.73 us
    ppermute x2, starting transfers between devices, padded(): lax.ppermute(lax.slice_in_dim(block, 0, width, axis=dim), axis, backward)  2.58 us
  transfers between devices with their start and end apart: 4, of which 2 were waited for; matrix products, arithmetic and copies ran while one was open for 1% of the time, Pallas kernels for 0%

profile of v1, /device:TPU:0, one launch (start us, length us, event | category | flops | bytes accessed | tf_op | source)
XLA Modules:
  0.0 96.3 jit_solution(578989665195896975)
XLA Ops:
  0.6 0.0 copy-start.6
  0.6 0.0 copy-start.8
  0.7 0.0 copy-start.9
  0.7 0.0 copy-start.7
  0.7 0.0 copy-start.10
  0.7 0.0 copy-start.3
  0.7 1.3 %dynamic_slice.3 = s32[1,1]{1,0:T(1,128)} dynamic-slice(s32[4,4]{1,0:T(4,128)} %param.16, s32[]{:T(128)S(6)} %select_n.24, s32[]{:T(128)S(6)} %select_n.25), dynamic_slice_sizes={1,1} | dynamic-slice | bytes 12 | tf_op jit(solution)/shard_map/dynamic_slice | solution.py:368
  2.6 0.0 copy-start
  2.7 1.6 %copy-done = bf16[32,1,9,3840]{3,0,2,1:T(8,128)(2,1)S(1)} copy-done((bf16[32,1,9,3840]{3,0,2,1:T(8,128)(2,1)S(1)}, bf16[32,1,9,3840]{3,0,2,1:T(8,128)(2,1)}, u32[]{:S(2)}) %copy-start) | copy-done | bytes 2211864
  4.3 0.0 copy-start.4
  4.3 0.0 copy-start.1
  4.3 0.0 copy-start.2
  4.3 55.1 %frame_sims.1 = f32[4,32,128]{2,1,0:T(8,128)S(1)} custom-call(bf16[1152,3840]{1,0:T(8,128)(2,1)} %bitcast.40, bf16[288,3840]{1,0:T(8,128)(2,1)S(1)} %bitcast.36), custom_call_target="tpu_custom_call" | custom-call | tf_op jit(solution)/shard_map/frame_sims/pallas_call | solution.py:164
  59.4 3.5 %collective-permute-start = (f32[8,128]{1,0:T(8,128)S(1)}, f32[8,128]{1,0:T(8,128)S(1)}, u32[]{:S(2)}, u32[]{:S(2)}) collective-permute-start(f32[8,128]{1,0:T(8,128)S(1)} %bitcast.43), channel_id=1, source_target_pairs={{0,1},{1,2},{2,3},{4,5},{5,6},{6,7},{8,9},{9,10},{10,11},{12,13},{... | collective-permute-start | bytes 12296 | tf_op jit(solution)/shard_map/ppermute | solution.py:349
  62.9 1.3 %collective-permute-start.1 = (f32[8,128]{1,0:T(8,128)S(1)}, f32[8,128]{1,0:T(8,128)S(1)}, u32[]{:S(2)}, u32[]{:S(2)}) collective-permute-start(f32[8,128]{1,0:T(8,128)S(1)} %bitcast.44), channel_id=1, source_target_pairs={{1,0},{2,1},{3,2},{5,4},{6,5},{7,6},{9,8},{10,9},{11,10},{13,12},{... | collective-permute-start | bytes 12296 | tf_op jit(solution)/shard_map/ppermute | solution.py:352
  64.2 0.0 copy-done.6
  64.2 0.0 copy-done.4
  64.3 0.4 fusion.4
  64.7 0.2 reshape.125
  64.9 0.0 copy-done.8
  64.9 0.0 copy-done.9
  65.0 0.2 reduce-window.8
  65.8 0.1 compare_and_fusion
  65.9 0.0 collective-permute-done
  66.0 2.5 %collective-permute-done.1 = f32[8,128]{1,0:T(8,128)S(1)} collective-permute-done((f32[8,128]{1,0:T(8,128)S(1)}, f32[8,128]{1,0:T(8,128)S(1)}, u32[]{:S(2)}, u32[]{:S(2)}) %collective-permute-start.1) | collective-permute-done | bytes 4128 | tf_op jit(solution)/shard_map/ppermute | solution.py:352
  68.4 0.1 fusion.2
  68.5 1.3 %collective-permute-start.2 = (f32[144,8]{1,0:T(8,128)S(1)}, f32[144,8]{1,0:T(8,128)S(1)}, u32[]{:S(2)}, u32[]{:S(2)}) collective-permute-start(f32[144,8]{1,0:T(8,128)S(1)} %get-tuple-element.10), channel_id=1, source_target_pairs={{0,4},{4,8},{8,12},{1,5},{5,9},{9,13},{2,6},{6,10},{10,14},{3,7},{... | collective-permute-start | bytes 13832 | tf_op jit(solution)/shard_map/ppermute | solution.py:349
  69.8 1.3 %collective-permute-start.3 = (f32[144,8]{1,0:T(8,128)S(1)}, f32[144,8]{1,0:T(8,128)S(1)}, u32[]{:S(2)}, u32[]{:S(2)}) collective-permute-start(f32[144,8]{1,0:T(8,128)S(1)} %get-tuple-element.11), channel_id=1, source_target_pairs={{4,0},{8,4},{12,8},{5,1},{9,5},{13,9},{6,2},{10,6},{14,10},{7,3},{... | collective-permute-start | bytes 13832 | tf_op jit(solution)/shard_map/ppermute | solution.py:352
  71.1 0.1 pad_add_fusion.where_ref
  71.2 0.0 copy-done.7
  71.2 0.1 broadcast_in_dim_tile.6.b1_ref
  71.3 0.0 copy-done.10
  71.3 0.1 broadcast_in_dim_tile.7.b2_ref
  72.0 0.0 collective-permute-done.2
  72.0 2.2 %collective-permute-done.3 = f32[144,8]{1,0:T(8,128)S(1)} collective-permute-done((f32[144,8]{1,0:T(8,128)S(1)}, f32[144,8]{1,0:T(8,128)S(1)}, u32[]{:S(2)}, u32[]{:S(2)}) %collective-permute-start.3) | collective-permute-done | bytes 4640 | tf_op jit(solution)/shard_map/ppermute | solution.py:352
  74.3 0.1 pad_maximum_fusion.map_ref
  74.4 0.0 copy-done.3
  74.4 0.0 copy-done.1
  74.4 0.0 copy-done.2
  74.4 3.7 %network.1 = f32[36,40]{1,0:T(8,128)S(1)} custom-call(s32[4]{0:T(128)S(1)} %pad_add_fusion.where_ref, f32[144,144]{1,0:T(8,128)S(1)} %pad_maximum_fusion.map_ref, bf16[144,512]{1,0:T(8,128)(2,1)S(1)} %pad_maximum_fusion.1.w1_ref, f32[1,128]{1,0:T(1,128)S(1)} %broadcast_in_dim_tile.6.b1_ref, bf16[9,32,64]{2,1,0:T(8,128)(2,1)S(1)} %bitcast.38, ...), custom_call_target="tpu_custom_call" | custom-call | tf_op jit(solution)/shard_map/network/pallas_call | solution.py:316
  78.2 0.1 fusion.1
  78.3 0.1 copy.33
  78.3 0.0 copy-start.5
  78.3 0.1 select_reduce_fusion
  78.4 10.6 %pmax.7 = f32[32,2]{0,1:T(2,128)S(1)} all-reduce(f32[32,2]{0,1:T(2,128)S(1)} %select_reduce_fusion), channel_id=1, replica_groups=mesh['groups'=2,'qry'=4,'ref'=4] {'ref'}, use_global_device_ids=true, to_apply=%region_2.3 | all-reduce | flops 64 | bytes 512 | tf_op jit(solution)/shard_map/pmax | solution.py:391
  89.0 0.1 select_reduce_fusion.1
  89.1 6.6 %psum.7 = f32[2]{0:T(128)S(1)} all-reduce(f32[2]{0:T(128)S(1)} %select_reduce_fusion.1), channel_id=1, replica_groups=mesh['groups'=2,'qry'=4,'ref'=4] {'qry'}, use_global_device_ids=true, to_apply=%region_4.5 | all-reduce | flops 2 | bytes 16 | tf_op jit(solution)/shard_map/psum | solution.py:394
  95.8 0.5 broadcast_divide_fusion
  96.3 0.0 copy-done.5
  (16 shorter events, 0.1 us)
Async XLA Ops:
  0.6 63.6 %copy-start.6 = (f32[3,3,32]{2,1,0:T(4,128)S(1)}, f32[3,3,32]{2,1,0:T(4,128)}, u32[]{:S(2)}) copy-start(f32[3,3,32]{2,1,0:T(4,128)} %param.19) | copy-start | bytes 3460
  0.6 64.3 %copy-start.8 = (bf16[128]{0:T(256)(128)(2,1)S(1)}, bf16[128]{0:T(256)(128)(2,1)}, u32[]{:S(2)}) copy-start(bf16[128]{0:T(256)(128)(2,1)} %param.25) | copy-start | bytes 772
  0.7 64.3 %copy-start.9 = (s32[2]{0:T(128)S(1)}, s32[2]{0:T(128)}, u32[]{:S(2)}) copy-start(s32[2]{0:T(128)} %param.17) | copy-start | bytes 28
  0.7 70.5 %copy-start.7 = (f32[32]{0:T(128)S(1)}, f32[32]{0:T(128)}, u32[]{:S(2)}) copy-start(f32[32]{0:T(128)} %param.20) | copy-start | bytes 388
  0.7 70.6 %copy-start.10 = (f32[64]{0:T(128)S(1)}, f32[64]{0:T(128)}, u32[]{:S(2)}) copy-start(f32[64]{0:T(128)} %param.22) | copy-start | bytes 772
  0.7 73.7 %copy-start.3 = (f32[128]{0:T(128)S(1)}, f32[128]{0:T(128)}, u32[]{:S(2)}) copy-start(f32[128]{0:T(128)} %param.24) | copy-start | bytes 1540
  2.6 1.6 %copy-start = (bf16[32,1,9,3840]{3,0,2,1:T(8,128)(2,1)S(1)}, bf16[32,1,9,3840]{3,0,2,1:T(8,128)(2,1)}, u32[]{:S(2)}) copy-start(bf16[32,1,9,3840]{3,0,2,1:T(8,128)(2,1)} %param.15) | copy-start | bytes 6635524
  4.3 60.0 %copy-start.4 = (f32[768,9]{1,0:T(8,128)S(1)}, f32[768,9]{1,0:T(8,128)}, u32[]{:S(2)}) copy-start(f32[768,9]{1,0:T(8,128)} %constant.26.clone) | copy-start | bytes 82948
  4.3 70.2 %copy-start.1 = (bf16[3,3,128,64]{2,3,1,0:T(8,128)(2,1)S(1)}, bf16[3,3,128,64]{2,3,1,0:T(8,128)(2,1)}, u32[]{:S(2)}) copy-start(bf16[3,3,128,64]{2,3,1,0:T(8,128)(2,1)} %param.23) | copy-start | bytes 442372
  4.3 70.2 %copy-start.2 = (bf16[3,3,64,32]{2,3,1,0:T(8,128)(2,1)S(1)}, bf16[3,3,64,32]{2,3,1,0:T(8,128)(2,1)}, u32[]{:S(2)}) copy-start(bf16[3,3,64,32]{2,3,1,0:T(8,128)(2,1)} %param.21) | copy-start | bytes 110596
  59.4 6.5 %collective-permute-start = (f32[8,128]{1,0:T(8,128)S(1)}, f32[8,128]{1,0:T(8,128)S(1)}, u32[]{:S(2)}, u32[]{:S(2)}) collective-permute-start(f32[8,128]{1,0:T(8,128)S(1)} %bitcast.43), channel_id=1, source_target_pairs={{0,1},{1,2},{2,3},{4,5},{5,6},{6,7},{8,9},{9,10},{10,11},{12,13},{... | collective-permute-start | bytes 12296 | tf_op jit(solution)/shard_map/ppermute | solution.py:349
  62.9 5.5 %collective-permute-start.1 = (f32[8,128]{1,0:T(8,128)S(1)}, f32[8,128]{1,0:T(8,128)S(1)}, u32[]{:S(2)}, u32[]{:S(2)}) collective-permute-start(f32[8,128]{1,0:T(8,128)S(1)} %bitcast.44), channel_id=1, source_target_pairs={{1,0},{2,1},{3,2},{5,4},{6,5},{7,6},{9,8},{10,9},{11,10},{13,12},{... | collective-permute-start | bytes 12296 | tf_op jit(solution)/shard_map/ppermute | solution.py:352
  68.5 3.5 %collective-permute-start.2 = (f32[144,8]{1,0:T(8,128)S(1)}, f32[144,8]{1,0:T(8,128)S(1)}, u32[]{:S(2)}, u32[]{:S(2)}) collective-permute-start(f32[144,8]{1,0:T(8,128)S(1)} %get-tuple-element.10), channel_id=1, source_target_pairs={{0,4},{4,8},{8,12},{1,5},{5,9},{9,13},{2,6},{6,10},{10,14},{3,7},{... | collective-permute-start | bytes 13832 | tf_op jit(solution)/shard_map/ppermute | solution.py:349
  69.8 4.5 %collective-permute-start.3 = (f32[144,8]{1,0:T(8,128)S(1)}, f32[144,8]{1,0:T(8,128)S(1)}, u32[]{:S(2)}, u32[]{:S(2)}) collective-permute-start(f32[144,8]{1,0:T(8,128)S(1)} %get-tuple-element.11), channel_id=1, source_target_pairs={{4,0},{8,4},{12,8},{5,1},{9,5},{13,9},{6,2},{10,6},{14,10},{7,3},{... | collective-permute-start | bytes 13832 | tf_op jit(solution)/shard_map/ppermute | solution.py:352
  78.3 18.0 %copy-start.5 = (f32[32,32]{1,0:T(8,128)}, f32[32,32]{1,0:T(8,128)S(1)}, u32[]{:S(2)}) copy-start(f32[32,32]{1,0:T(8,128)S(1)} %copy.33) | copy-start | bytes 12292

commit v2 on v1

--- a/solution.py
+++ b/solution.py
@@ -15,9 +15,13 @@
 LEAD = 48
 
 
-def sims_kernel(
-    chips, regions, frames, scale, chunk, q_hbm, r_hbm, out_ref, q_buf, r_buf, acc,
-    q_sem, own_sem, send_x, recv_x, send_s, recv_s,
+def whole_kernel(
+    chips, others, regions, frames, scale, chunk, pair_ref, lengths_ref, len_ref, b4_ref,
+    w1_ref, b1_ref, w2_ref, b2_ref, w3_ref, b3_ref, w4_ref, q_hbm, r_hbm,
+    scores_ref, totals_ref,
+    q_buf, r_buf, acc, sims_buf, map_buf, z_buf, x_buf, first_buf, second_buf, w2_full, w3_full,
+    peaks_buf, sums_buf,
+    q_sem, own_sem, send_x, recv_x, send_s, recv_s, send_h, recv_h, send_p, recv_p, send_t, recv_t,
 ):
     depth = r_hbm.shape[1]
     steps = depth // chunk
@@ -28,7 +32,12 @@
     core = me % 2
     sibling = chip * 2 + (1 - core)
     right = ((chip + 1) % chips) * 2 + core
-    left = ((chip + chips - 1) % chips) * 2 + core
+    senders = 2 * chips
+    col = lax.axis_index("ref")
+
+    def reachable(move_q, move_r):
+        fits = (me + move_q >= 0) & (me + move_q < senders)
+        return fits & (col + move_r >= 0) & (col + move_r < others)
 
     def cols(c):
         return pl.ds(pl.multiple_of(c * chunk, 128), chunk)
@@ -69,11 +78,19 @@
         return carry
 
     lax.fori_loop(0, steps, start_own, 0)
+    map_buf[...] = jnp.zeros_like(map_buf)
     barrier = pltpu.get_barrier_semaphore()
-    greet = (sibling, right) if chips == 2 else (sibling, right, left)
-    for device in greet:
-        pl.semaphore_signal(barrier, inc=1, device_id={"qry": device}, device_id_type=MESH)
-    pl.semaphore_wait(barrier, len(greet))
+    for k in range(1, senders):
+        device = {"qry": (me + k) % senders}
+        pl.semaphore_signal(barrier, inc=1, device_id=device, device_id_type=MESH)
+    for k in range(1, others):
+        device = {"ref": (col + k) % others}
+        pl.semaphore_signal(barrier, inc=1, device_id=device, device_id_type=MESH)
+    for move_q in (1, senders - 1):
+        for move_r in (1, others - 1):
+            device = {"qry": (me + move_q) % senders, "ref": (col + move_r) % others}
+            pl.semaphore_signal(barrier, inc=1, device_id=device, device_id_type=MESH)
+    pl.semaphore_wait(barrier, senders - 1 + others - 1 + 4)
 
     def start_sends(c, carry):
         to_right(0, c).start()
@@ -105,9 +122,11 @@
             best = jnp.max(acc[side, i].reshape(regions, shard, 384), axis=0)
             for k in range(384 // frames):
                 total = total + best[:, k * frames : (k + 1) * frames]
-        out_ref[source] = total * scale
-
+        sims_buf[source] = total * (scale * active)
+
+    active = pair_ref[me, col].astype(jnp.float32)
     acc[...] = jnp.zeros_like(acc)
+    build_weights(w2_ref, w3_ref, w2_full, w3_full)
 
     def first_own(c, carry):
         own_copy(c).wait()
@@ -150,51 +169,104 @@
 
     lax.fori_loop(0, steps, drain, 0)
 
-
-def frame_sims(query_mat, ref_mat, regions, senders):
-    depth = query_mat.shape[1]
-    frames = query_mat.shape[0] // regions
-    rows = ref_mat.shape[0]
-    shard = rows // regions
-    chips = senders // 2
-    chunk = 768 if depth % 768 == 0 else depth
-    steps = depth // chunk
-    parts = regions * frames // 384
-    scale = 1.0 / (regions * math.sqrt(depth))
-    return pl.pallas_call(
-        functools.partial(sims_kernel, chips, regions, frames, scale, chunk),
-        out_shape=jax.ShapeDtypeStruct((senders, shard, frames), jnp.float32),
-        in_specs=[pl.BlockSpec(memory_space=pl.ANY)] * 2,
-        out_specs=pl.BlockSpec(memory_space=pltpu.VMEM),
-        scratch_shapes=[
-            pltpu.VMEM(query_mat.shape, jnp.bfloat16),
-            pltpu.VMEM((senders, rows, depth), jnp.bfloat16),
-            pltpu.VMEM((2, parts, rows, 384), jnp.float32),
-            pltpu.SemaphoreType.DMA((steps,)),
-            pltpu.SemaphoreType.DMA((steps,)),
-            pltpu.SemaphoreType.DMA((chips, steps)),
-            pltpu.SemaphoreType.DMA((chips, steps)),
-            pltpu.SemaphoreType.DMA((chips, steps)),
-            pltpu.SemaphoreType.DMA((chips, steps)),
-        ],
-        compiler_params=pltpu.CompilerParams(
-            collective_id=0, has_side_effects=True, vmem_limit_bytes=48 << 20
-        ),
-        name="frame_sims",
-    )(query_mat, ref_mat)
-
-
-def net_kernel(
-    tiles_p, tiles_f, where_ref, map_ref, w1_ref, b1_ref, w2_ref, b2_ref, w3_ref, b3_ref,
-    w4_ref, out_ref, z_buf, x_buf, first_buf, second_buf, w2_full, w3_full,
-):
-    side = tiles_p + 4
-    rows = side * PITCH
-    wide = map_ref.shape[0]
-    lane = lax.broadcasted_iota(jnp.int32, (1, 128), 1)
-    low_a = lane < 64
-    low_b = (lane % 64) < 32
-
+    for b in range(senders):
+        map_buf.at[1][pl.ds(HALO + b, shard, stride=senders), :] = sims_buf[b]
+
+    def halo_copy(k, move_q, move_r):
+        if move_r == 0:
+            source, target = pl.ds(HALO, frames), pl.ds(HALO, frames)
+        elif move_r == 1:
+            source, target = pl.ds(frames, HALO), pl.ds(0, HALO)
+        else:
+            source, target = pl.ds(HALO, HALO), pl.ds(HALO + frames, HALO)
+        return pltpu.make_async_remote_copy(
+            src_ref=map_buf.at[1, source],
+            dst_ref=map_buf.at[1 - move_q, target],
+            send_sem=send_h.at[k],
+            recv_sem=recv_h.at[k],
+            device_id={"qry": me + move_q, "ref": col + move_r},
+            device_id_type=MESH,
+        )
+
+    moves = [(q, r) for q in (-1, 1, 0) for r in (-1, 1, 0) if (q, r) != (0, 0)]
+    for k, (move_q, move_r) in enumerate(moves):
+
+        @pl.when(reachable(move_q, move_r))
+        def _():
+            halo_copy(k, move_q, move_r).start()
+
+    for k, (move_q, move_r) in enumerate(moves):
+
+        @pl.when(reachable(-move_q, -move_r))
+        def _():
+            halo_copy(k, move_q, move_r).wait_recv()
+
+    for k, (move_q, move_r) in enumerate(moves):
+
+        @pl.when(reachable(move_q, move_r))
+        def _():
+            halo_copy(k, move_q, move_r).wait_send()
+
+    tiles = frames // 4
+    scores = network(
+        tiles, (me * tiles, col * tiles, senders * tiles, others * tiles), map_buf, w1_ref, b1_ref,
+        b2_ref, b3_ref, w4_ref, z_buf, x_buf, first_buf, second_buf, w2_full, w3_full,
+    ) + b4_ref[0]
+    scores_ref[...] = scores
+    slot_f = lax.broadcasted_iota(jnp.int32, scores.shape, 0)
+    column = slot_f + (col * tiles - 2)
+    own = (slot_f >= 2) & (slot_f < 2 + tiles)
+    peaks_buf[0] = jnp.zeros_like(peaks_buf[0])
+    begin = jnp.int32(0)
+    for v in range(lengths_ref.shape[0]):
+        end = begin + lengths_ref[v]
+        member = own & (column >= begin) & (column < end)
+        peaks_buf[0, v : v + 1, :PITCH] = jnp.max(
+            jnp.where(member, scores, -jnp.inf), axis=0, keepdims=True
+        )
+        begin = end
+
+    def peak_copy(k):
+        return pltpu.make_async_remote_copy(
+            src_ref=peaks_buf.at[0],
+            dst_ref=peaks_buf.at[k],
+            send_sem=send_p.at[k],
+            recv_sem=recv_p.at[k],
+            device_id={"ref": (col + k) % others},
+            device_id_type=MESH,
+        )
+
+    def sum_copy(k):
+        return pltpu.make_async_remote_copy(
+            src_ref=sums_buf.at[0],
+            dst_ref=sums_buf.at[k],
+            send_sem=send_t.at[k],
+            recv_sem=recv_t.at[k],
+            device_id={"qry": (me + k) % senders},
+            device_id_type=MESH,
+        )
+
+    for k in range(1, others):
+        peak_copy(k).start()
+    for k in range(1, others):
+        peak_copy(k).wait_recv()
+    peaks = jnp.max(peaks_buf[...], axis=0)
+    lane = lax.broadcasted_iota(jnp.int32, peaks.shape, 1)
+    counted = (lane >= 2) & (lane < 2 + tiles) & (lane + (me * tiles - 2) < len_ref[0])
+    partial_sum = jnp.sum(jnp.where(counted, peaks, 0.0), axis=1, keepdims=True)
+    sums_buf[0] = jnp.broadcast_to(partial_sum, peaks.shape)
+    for k in range(1, senders):
+        sum_copy(k).start()
+    for k in range(1, senders):
+        sum_copy(k).wait_recv()
+    totals_ref[...] = jnp.sum(sums_buf[...], axis=0) / len_ref[0].astype(jnp.float32)
+    for k in range(1, others):
+        peak_copy(k).wait_send()
+    for k in range(1, senders):
+        sum_copy(k).wait_send()
+
+
+def build_weights(w2_ref, w3_ref, w2_full, w3_full):
     w2_full[...] = jnp.zeros_like(w2_full)
     taps = {(0, 0): 0, (0, 1): 1, (1, 0): 2, (1, 1): -1}
     for g in range(2):
@@ -213,14 +285,27 @@
         w3_full[k * 64 : (k + 1) * 64, :] = w3_ref[k]
     w3_full[576:640, :] = jnp.zeros((64, 128), jnp.bfloat16)
 
-    source = lax.broadcasted_iota(jnp.int32, (wide, 128), 0)
-    target = lax.broadcasted_iota(jnp.int32, (wide, 128), 1)
-    whole = map_ref[...]
+
+def network(
+    tiles, where_ref, map_ref, w1_ref, b1_ref, b2_ref, b3_ref, w4_ref,
+    z_buf, x_buf, first_buf, second_buf, w2_full, w3_full,
+):
+    side = tiles + 4
+    rows = side * PITCH
+    wide = map_ref.shape[1]
+    frames = map_ref.shape[2]
+    lane = lax.broadcasted_iota(jnp.int32, (1, 128), 1)
+    low_a = lane < 64
+    low_b = (lane % 64) < 32
+
+    source = lax.broadcasted_iota(jnp.int32, (3 * frames, 128), 0)
+    target = lax.broadcasted_iota(jnp.int32, (3 * frames, 128), 1)
+    whole = jnp.concatenate([map_ref[0], map_ref[1], map_ref[2]], axis=1)
     high = whole.astype(jnp.bfloat16)
     lower = (whole - high.astype(jnp.float32)).astype(jnp.bfloat16)
     z_buf[...] = jnp.zeros_like(z_buf)
     for rr in range(6):
-        pick = jnp.where(source == 4 * target - 1 + rr, 1.0, 0.0).astype(jnp.bfloat16)
+        pick = jnp.where(source == 4 * target + (frames - 9) + rr, 1.0, 0.0).astype(jnp.bfloat16)
         for part, value in enumerate((high, lower)):
             z_buf[part, 8 : 8 + wide, rr * 128 : (rr + 1) * 128] = jnp.dot(
                 value, pick, preferred_element_type=jnp.float32
@@ -287,7 +372,7 @@
     made = jnp.dot(stacked, w3_full[...], preferred_element_type=jnp.float32)
     third = jnp.maximum(made + b3_ref[...], 0.0).astype(jnp.bfloat16).astype(jnp.float32)
     weighted = third * w4_ref[...]
-    out_ref[...] = jnp.sum(weighted.reshape(side, PITCH, 128), axis=2)
+    return jnp.sum(weighted.reshape(side, PITCH, 128), axis=2)
 
 
 def first_matrix(weight):
@@ -307,92 +392,90 @@
     return jnp.concatenate([high, high, full - high], axis=0).astype(jnp.bfloat16)
 
 
-def network(
-    wide_map, where, tiles, w1, b1, w2, b2, w3, b3, w4
+def body(
+    query_feats, ref_feats, pair_table, lengths, query_len, conv1_weight, conv1_bias,
+    conv2_weight, conv2_bias, conv3_weight, conv3_bias, conv4_weight, conv4_bias,
 ):
+    senders = lax.axis_size("qry")
+    others = lax.axis_size("ref")
+    frames, regions, depth = query_feats.shape
+    query_mat = jnp.transpose(query_feats, (1, 0, 2)).reshape(regions * frames, depth)
+    ref_mat = jnp.transpose(ref_feats, (1, 2, 0, 3)).reshape(-1, depth)
+    videos = lengths.shape[0]
+    video_rows = -(-videos // 8) * 8
+    shard_rows = ref_mat.shape[0]
+    chips = senders // 2
+    chunk = 256 if depth % 256 == 0 else depth
+    steps = depth // chunk
+    parts = regions * frames // 384
+    tiles = frames // 4
     side = tiles + 4
     rows = side * PITCH
+    scale = 1.0 / (regions * math.sqrt(depth))
     vmem = pl.BlockSpec(memory_space=pltpu.VMEM)
-    return pl.pallas_call(
-        functools.partial(net_kernel, tiles, tiles),
-        out_shape=jax.ShapeDtypeStruct((side, PITCH), jnp.float32),
-        in_specs=[pl.BlockSpec(memory_space=pltpu.SMEM)] + [vmem] * 8,
-        out_specs=vmem,
+    smem = pl.BlockSpec(memory_space=pltpu.SMEM)
+    hbm = pl.BlockSpec(memory_space=pl.ANY)
+    dma = pltpu.SemaphoreType.DMA
+    scores, totals = pl.pallas_call(
+        functools.partial(whole_kernel, chips, others, regions, frames, scale, chunk),
+        out_shape=(
+            jax.ShapeDtypeStruct((side, PITCH), jnp.float32),
+            jax.ShapeDtypeStruct((video_rows, 128), jnp.float32),
+        ),
+        in_specs=[smem] * 4 + [vmem] * 7 + [hbm] * 2,
+        out_specs=(vmem, vmem),
         scratch_shapes=[
-            pltpu.VMEM((2, wide_map.shape[0] + 16, 768), jnp.float32),
+            pltpu.VMEM(query_mat.shape, jnp.bfloat16),
+            pltpu.VMEM((senders, shard_rows, depth), jnp.bfloat16),
+            pltpu.VMEM((2, parts, shard_rows, 384), jnp.float32),
+            pltpu.VMEM((senders, frames // senders, frames), jnp.float32),
+            pltpu.VMEM((3, frames + 2 * HALO, frames), jnp.float32),
+            pltpu.VMEM((2, frames + 4 * HALO, 768), jnp.float32),
             pltpu.VMEM((rows, 144), jnp.float32),
             pltpu.VMEM((rows + 2 * LEAD, 128), jnp.float32),
             pltpu.VMEM((rows + 2 * LEAD, 128), jnp.float32),
             pltpu.VMEM((512, 256), jnp.bfloat16),
             pltpu.VMEM((640, 128), jnp.bfloat16),
+            pltpu.VMEM((others, video_rows, 128), jnp.float32),
+            pltpu.VMEM((senders, video_rows, 128), jnp.float32),
+            dma((steps,)),
+            dma((steps,)),
+            dma((chips, steps)),
+            dma((chips, steps)),
+            dma((chips, steps)),
+            dma((chips, steps)),
+            dma((8,)),
+            dma((8,)),
+            dma((others,)),
+            dma((others,)),
+            dma((senders,)),
+            dma((senders,)),
         ],
-        compiler_params=pltpu.CompilerParams(vmem_limit_bytes=48 << 20),
-        name="network",
+        compiler_params=pltpu.CompilerParams(
+            collective_id=0, has_side_effects=True, vmem_limit_bytes=56 << 20
+        ),
+        name="whole",
     )(
-        where,
-        wide_map,
-        w1,
-        jnp.tile(b1, 4)[None],
-        jnp.transpose(w2, (0, 1, 3, 2)).reshape(9, w2.shape[3], w2.shape[2]),
-        jnp.tile(b2, 2)[None],
-        jnp.transpose(w3, (0, 1, 3, 2)).reshape(9, w3.shape[3], w3.shape[2]),
-        b3[None],
-        w4.astype(jnp.float32)[None],
-    )
-
-
-def padded(block, sides, width):
-    for axis, dim in sides:
-        count = lax.axis_size(axis)
-        forward = [(i, i + 1) for i in range(count - 1)]
-        backward = [(target, source) for source, target in forward]
-        low = lax.ppermute(
-            lax.slice_in_dim(block, block.shape[dim] - width, None, axis=dim), axis, forward
-        )
-        high = lax.ppermute(lax.slice_in_dim(block, 0, width, axis=dim), axis, backward)
-        block = jnp.concatenate([low, block, high], axis=dim)
-    return block
-
-
-def body(
-    query_feats, ref_feats, pair_table, lengths, query_len, conv1_weight, conv1_bias,
-    conv2_weight, conv2_bias, conv3_weight, conv3_bias, conv4_weight, conv4_bias,
-):
-    qry_index = lax.axis_index("qry")
-    ref_index = lax.axis_index("ref")
-    senders = lax.axis_size("qry")
-    frames, regions, channels = query_feats.shape
-    query_mat = jnp.transpose(query_feats, (1, 0, 2)).reshape(regions * frames, channels)
-    ref_mat = jnp.transpose(ref_feats, (1, 2, 0, 3)).reshape(-1, channels)
-    sims = frame_sims(query_mat, ref_mat, regions, senders)
-    active = lax.dynamic_slice(pair_table, (qry_index, ref_index), (1, 1)) == 1
-    sims = jnp.transpose(sims, (1, 0, 2)).reshape(frames, frames)
-    sims = jnp.where(active, sims, 0.0)
-    wide_map = padded(sims, (("ref", 0), ("qry", 1)), HALO)
-    tiles = frames // 4
-    where = jnp.stack(
-        [
-            qry_index * tiles,
-            ref_index * tiles,
-            jnp.int32(senders * tiles),
-            jnp.int32(lax.axis_size("ref") * tiles),
-        ]
-    ).astype(jnp.int32)
-    scores = network(
-        wide_map, where, tiles, first_matrix(conv1_weight), conv1_bias, conv2_weight,
-        conv2_bias, conv3_weight, conv3_bias, conv4_weight,
-    )
-    score_map = jnp.transpose(scores[2 : 2 + tiles, 2 : 2 + tiles]) + conv4_bias[0]
-    ends = jnp.cumsum(lengths)
-    starts = ends - lengths
-    column = ref_index * tiles + jnp.arange(tiles, dtype=jnp.int32)
-    member = (column[:, None] >= starts[None, :]) & (column[:, None] < ends[None, :])
-    peaks = jnp.max(jnp.where(member[None], score_map[:, :, None], -jnp.inf), axis=1)
-    peaks = lax.pmax(peaks, "ref")
-    row_ids = qry_index * tiles + jnp.arange(tiles, dtype=jnp.int32)
-    partial_value = jnp.sum(jnp.where((row_ids < query_len[0])[:, None], peaks, 0.0), axis=0)
-    totals = lax.psum(partial_value, "qry")
-    return (score_map, totals / query_len[0].astype(jnp.float32))
+        pair_table,
+        lengths,
+        query_len,
+        conv4_bias,
+        first_matrix(conv1_weight),
+        jnp.tile(conv1_bias, 4)[None],
+        jnp.transpose(conv2_weight, (0, 1, 3, 2)).reshape(
+            9, conv2_weight.shape[3], conv2_weight.shape[2]
+        ),
+        jnp.tile(conv2_bias, 2)[None],
+        jnp.transpose(conv3_weight, (0, 1, 3, 2)).reshape(
+            9, conv3_weight.shape[3], conv3_weight.shape[2]
+        ),
+        conv3_bias[None],
+        conv4_weight.astype(jnp.float32)[None],
+        query_mat,
+        ref_mat,
+    )
+    score_map = jnp.transpose(scores[2 : 2 + tiles, 2 : 2 + tiles])
+    return (score_map, totals[:videos, 0])
 
 
 def solution(mesh):

time: 96.6 us -> 86.2 us (0.89)
  blocking collectives: 17.2 us -> 0 us
  Pallas kernels: 58.8 us -> 74.4 us
  starting transfers between devices: 7.35 us -> 0 us
  waiting for transfers between devices: 4.71 us -> 0 us
  local copies, waits for them, and re-layouts: 3.53 us -> 6.17 us
  matrix products: 0.44 us -> 1.45 us
    pallas_call x2 -> x1, Pallas kernels: 58.8 us -> 74.4 us  [body(): pl.pallas_call(functools.partial(whole_kernel, chips, others, regions, fr...]
    pmax x1 -> x0, blocking collectives: 10.6 us -> none  [body(): peaks = lax.pmax(peaks, 'ref')]
    ppermute x4 -> x0, starting transfers between devices: 7.35 us -> none  [the longest x2 4.76 us: padded(): lax.ppermute(lax.slice_in_dim(block, block.shape[dim] - width, None, axis...]
    psum x1 -> x0, blocking collectives: 6.64 us -> none  [body(): totals = lax.psum(partial_value, 'qry')]
    ppermute x4 -> x0, waiting for transfers between devices: 4.71 us -> none  [the longest x2 4.7 us: padded(): lax.ppermute(lax.slice_in_dim(block, 0, width, axis=dim), axis, backward)]
    another operation x5 -> x4, local copies, waits for them, and re-layouts: 0.18 us -> 2.5 us  [the longest x2 1.25 us: body(): jnp.tile(conv1_bias, 4)[None]]
    dynamic_slice x1 -> x0, local copies, waits for them, and re-layouts: 1.29 us -> none  [body(): active = lax.dynamic_slice(pair_table, (qry_index, ref_index), (1, 1)) == 1]
    broadcast_in_dim x1, other arithmetic: 0.01 us -> 1.23 us  [body(): conv4_weight.astype(jnp.float32)[None]]
  transfers between devices with their start and end apart: 4 -> 0, of which waited for: 2 -> 0; matrix products, arithmetic and copies ran while one was open for 1% -> 0% of each run, Pallas kernels for 0% -> 0%
where the time goes in v2:
time: 86.2 us; the launch traced here: 85.8 us
  Pallas kernels  74.4 us (86%)
  local copies, waits for them, and re-layouts  6.17 us (7%)
  between operations  1.95 us (2%)
  other arithmetic  1.91 us (2%)
  matrix products  1.45 us (2%)
    pallas_call x1, Pallas kernels, body(): pl.pallas_call(functools.partial(whole_kernel, chips, others, regions, fr...  74.4 us

profile of v2, /device:TPU:0, one launch (start us, length us, event | category | flops | bytes accessed | tf_op | source)
XLA Modules:
  0.0 85.8 jit_solution(11681865144311169362)
XLA Ops:
  0.6 0.7 reshape.24
  1.3 1.4 %fusion.1 = f32[768,32]{1,0:T(8,128)S(1)} fusion(f32[768,9]{1,0:T(8,128)} %constant.2.clone, f32[9,32]{1,0:T(8,128)S(1)} %reshape.24), kind=kOutput, calls=%fused_computation.7 | convolution fusion | flops 2654208 | bytes 127104 | tf_op jit(solution)/shard_map/dot_general | solution.py:388
  2.8 0.2 reshape.25
  3.0 0.7 pad_maximum_fusion.w1_ref
  3.7 0.7 tile.4
  4.3 0.6 broadcast_in_dim_tile.6.b1_ref
  4.9 0.7 tile.5
  5.6 0.6 broadcast_in_dim_tile.7.b2_ref
  6.2 1.2 %bitcast_convert_fusion.w4_ref = f32[1,128]{1,0:T(1,128)} fusion(bf16[128]{0:T(256)(128)(2,1)} %param.25), kind=kLoop, calls=%fused_computation.6 | loop fusion | flops 128 | bytes 768 | tf_op jit(solution)/shard_map/broadcast_in_dim | solution.py:473
  8.7 74.4 %whole.1 = (f32[36,40]{1,0:T(8,128)}, f32[8,128]{1,0:T(8,128)}) custom-call(s32[4,4]{1,0:T(4,128)} %pair_ref.1, s32[2]{0:T(128)} %lengths_ref.1, s32[1]{0:T(128)S(6)} %copy.21.len_ref, f32[1]{0:T(128)S(6)} %copy.22.b4_ref, bf16[144,512]{1,0:T(8,128)(2,1)} %pad_maximum_fusion.w1_ref, f32[1,128]{1,0:T(1,128)} %broadcast_in_dim_tile.6.b1_ref, ...), custom_call_target="tpu_custom_call" | custom-call | tf_op jit(solution)/shard_map/whole/pallas_call | solution.py:419
  83.0 0.8 slice_bitcast_fusion
  83.8 0.7 copy.19
  84.5 1.3 %slice_reduce_fusion = f32[2]{0:T(128)} fusion(f32[8,128]{1,0:T(8,128)} %get-tuple-element.5), kind=kLoop, calls=%fused_computation.5 | loop fusion | bytes 16 | tf_op jit(solution)/shard_map/slice | solution.py:478
  (1 shorter events, 0.0 us)
